TPU v7x, 32 devices: a whole 2x2x4 slice. The times are simulated.
32 devices in a mesh: groups: 2 (over x), rows: 8 (over z, y), chan: 2 (over core).
Axes of the slice: x: 2, y: 2, z: 4, core: 2. Of those that a mesh axis runs over, the one named last changes fastest.
Arguments:
- latents: bfloat16 [48, 32, 1024], P('groups', 'rows', 'chan'), parts along dimension 0, may hold values from -6 to 6
- timestep: int32 [6], P('groups'), parts along dimension 0, may hold values from 0 to 999
- label: int32 [6], P('groups'), parts along dimension 0, may hold values from 0 to 15
- time_table: bfloat16 [1000, 1024], P(None, 'chan'), may hold values from -3 to 3
- class_table: bfloat16 [16, 1024], replicated, may hold values from -6 to 6
- dw_kernel: bfloat16 [7, 7, 1024], P(None, None, 'chan'), may hold values from -0.875 to 0.875
- dw_bias: bfloat16 [1024], P('chan'), may hold values from -3 to 3
- ln_gain: bfloat16 [1024], P('chan'), may hold values from 0.25 to 1.75
- ln_bias: bfloat16 [1024], P('chan'), may hold values from -2 to 2
- up_weight: bfloat16 [1024, 4096], P(None, 'chan'), may hold values from -0.1875 to 0.1875
- up_bias: bfloat16 [4096], P('chan'), may hold values from -3 to 3
- down_weight: bfloat16 [4096, 1024], P('chan'), may hold values from -0.09375 to 0.09375
- down_bias: bfloat16 [1024], P('chan'), may hold values from -3 to 3
- layer_scale: bfloat16 [1024], replicated, may hold values from 0.5 to 1.5
Outputs:
- features: bfloat16 [48, 32, 1024], P(('groups', 'rows'), None, 'chan'), parts along dimension 0
- gradient: float32 [48, 32, 1024], P('groups', 'rows', 'chan'), parts along dimension 0
There are 2 independent parts, one for each index of `groups`. A program takes and returns all parts, laid end to end along the dimension named above; an argument that names none is the same for every part. Nothing has to cross between parts.
Inputs may be any that keep to these rules, and one draw needn't show every extreme that they name: One timestep index for each image, a row of the table of 1000 timesteps. `label`: one defect class for each image, out of 16 classes.
All inputs are finite; a program needn't handle non-finite values.
Results may differ from a plain program's by a relative error of at most 0.0045.
Values may be sent and summed in bfloat16 or wider, within the bound.
No kernel may reach another device: no remote copies, remote signals or barrier semaphores. Data moves between devices by JAX's collectives and lax.ppermute only.
A program may use at most 128 MiB of HBM per device.

v0:
```python
import jax
import jax.numpy as jnp
from jax import lax
from jax.sharding import PartitionSpec as P

KAPPA = 0.7978845608028654
EPSILON = 1e-06


def with_halo(cells, sides, width):
    for axis, dim in sides:
        count = lax.axis_size(axis)
        ends = count - 1
        head = lax.slice_in_dim(cells, 0, width, axis=dim)
        tail = lax.slice_in_dim(cells, cells.shape[dim] - width, cells.shape[dim], axis=dim)
        cells = jnp.concatenate(
            [
                lax.ppermute(tail, axis, [(i, (i + 1) % count) for i in range(ends)]),
                cells,
                lax.ppermute(head, axis, [((i + 1) % count, i) for i in range(ends)]),
            ],
            axis=dim,
        )
    return cells


def gelu_tanh(values):
    inner = KAPPA * (values + 0.044715 * values * values * values)
    return 0.5 * values * (1.0 + jnp.tanh(inner))


def gelu_slope(values):
    tangent = jnp.tanh(KAPPA * (values + 0.044715 * values * values * values))
    return 0.5 * (1.0 + tangent) + 0.5 * values * (1.0 - tangent * tangent) * KAPPA * (
        1.0 + 3.0 * 0.044715 * values * values
    )


def stencil(padded, kernel, masks):
    height = padded.shape[0] - 6
    width = padded.shape[1] - 6
    total = jnp.zeros((height, width, padded.shape[2]), jnp.float32)
    for row_tap in range(7):
        partial_row = jnp.zeros((height, width, padded.shape[2]), jnp.float32)
        for col_tap in range(7):
            partial_row = (
                partial_row
                + padded[row_tap : row_tap + height, col_tap : col_tap + width, :]
                * kernel[row_tap, col_tap]
            )
        total = total + partial_row * masks[row_tap][:, None, None]
    return total


def exact_dot(left, right):
    return jnp.dot(left, right, precision=lax.Precision.HIGHEST, preferred_element_type=jnp.float32)


def local_block(
    latent_pad,
    row_first,
    col_first,
    total_rows,
    total_cols,
    pad_grad,
    time_rows,
    class_half,
    slope_image,
    scale_half,
    dw_kernel,
    dw_bias,
    ln_gain,
    ln_bias,
    up_weight,
    up_bias,
    down_weight,
    down_bias,
    full_channels,
):
    pad_rows = latent_pad.shape[0]
    pad_cols = latent_pad.shape[1]
    height = pad_rows - 6
    width = pad_cols - 6
    channels = latent_pad.shape[2]
    images = time_rows.shape[0]
    image_height = total_rows // images
    row_global = row_first - 3 + jnp.arange(pad_rows, dtype=jnp.int32)
    row_image = jnp.floor_divide(row_global, image_height)
    col_global = col_first - 3 + jnp.arange(pad_cols, dtype=jnp.int32)
    col_valid = ((col_global >= 0) & (col_global < total_cols)).astype(jnp.float32)
    image_hot = (row_image[:, None] == jnp.arange(images, dtype=jnp.int32)[None, :]).astype(
        jnp.float32
    )
    time_pad = exact_dot(image_hot, time_rows)
    start_pad = latent_pad.astype(jnp.float32) + time_pad[:, None, :] * col_valid[None, :, None]
    masks = jnp.stack(
        [
            (row_image[tap : tap + height] == row_image[3 : 3 + height]).astype(jnp.float32)
            for tap in range(7)
        ]
    )
    kernel = dw_kernel.astype(jnp.float32)
    mixed = stencil(start_pad, kernel, masks) + dw_bias.astype(jnp.float32)
    tokens = height * width
    flat = mixed.reshape(tokens, channels)
    first_sum, second_sum = lax.psum((jnp.sum(flat, 1), jnp.sum(flat * flat, 1)), "chan")
    mean = first_sum / full_channels
    variance = second_sum / full_channels - mean * mean
    inverse = lax.rsqrt(variance + EPSILON)
    normed = (flat - mean[:, None]) * inverse[:, None]
    gain = ln_gain.astype(jnp.float32)
    scaled = (normed * gain + ln_bias.astype(jnp.float32)).astype(jnp.bfloat16)
    hidden = jnp.dot(
        lax.all_gather(scaled, "chan", axis=1, tiled=True),
        up_weight,
        preferred_element_type=jnp.float32,
    )
    hidden = hidden + up_bias.astype(jnp.float32)
    active = gelu_tanh(hidden).astype(jnp.bfloat16)
    branch = lax.psum_scatter(
        jnp.dot(active, down_weight, preferred_element_type=jnp.float32),
        "chan",
        scatter_dimension=1,
        tiled=True,
    )
    branch = branch + down_bias.astype(jnp.float32)
    start_cells = start_pad[3 : 3 + height, 3 : 3 + width].reshape(tokens, channels)
    features = (
        (start_cells + scale_half * branch).astype(jnp.bfloat16).reshape(height, width, channels)
    )
    token_image = image_hot[3 : 3 + height]
    slope_rows = exact_dot(token_image, slope_image)
    slope_tokens = jnp.broadcast_to(
        slope_rows[:, None, :], (height, width, slope_rows.shape[1])
    ).reshape(tokens, slope_rows.shape[1])
    hidden_grad = (slope_tokens * gelu_slope(hidden)).astype(jnp.bfloat16)
    grad_terms = lax.dot_general(
        hidden_grad, up_weight, (((1,), (1,)), ((), ())), preferred_element_type=jnp.float32
    )
    normed_grad = lax.psum_scatter(
        grad_terms.astype(jnp.bfloat16), "chan", scatter_dimension=1, tiled=True
    ).astype(jnp.float32)
    gained = normed_grad * gain
    grad_first, grad_second = lax.psum((jnp.sum(gained, 1), jnp.sum(gained * normed, 1)), "chan")
    mixed_grad = inverse[:, None] * (
        gained - grad_first[:, None] / full_channels - normed * grad_second[:, None] / full_channels
    )
    grad_pad = pad_grad(mixed_grad.reshape(height, width, channels))
    class_tokens = exact_dot(token_image, class_half)
    gradient = stencil(grad_pad, kernel[::-1, ::-1], masks) + class_tokens[:, None, :]
    return (features, gradient)


def per_device(
    latents,
    timestep,
    label,
    time_table,
    class_table,
    dw_kernel,
    dw_bias,
    ln_gain,
    ln_bias,
    up_weight,
    up_bias,
    down_weight,
    down_bias,
    layer_scale,
):
    channels = ln_gain.shape[0]
    full_channels = class_table.shape[1]
    half_index = lax.axis_index("chan")
    scale_full = layer_scale.astype(jnp.float32)
    scale_half = lax.dynamic_slice_in_dim(scale_full, half_index * channels, channels, 0)
    time_hot = (
        timestep[:, None] == jnp.arange(time_table.shape[0], dtype=jnp.int32)[None, :]
    ).astype(jnp.float32)
    time_rows = exact_dot(time_hot, time_table.astype(jnp.float32))
    class_hot = (
        label[:, None] == jnp.arange(class_table.shape[0], dtype=jnp.int32)[None, :]
    ).astype(jnp.float32)
    class_rows = exact_dot(class_hot, class_table.astype(jnp.float32))
    class_half = lax.dynamic_slice_in_dim(class_rows, half_index * channels, channels, 1)
    direction = (class_rows * scale_full).astype(jnp.bfloat16)
    slope_image = lax.dot_general(
        direction, down_weight, (((1,), (1,)), ((), ())), preferred_element_type=jnp.float32
    )
    latent_rows = lax.all_to_all(latents, "rows", split_axis=0, concat_axis=1, tiled=True)
    height = latent_rows.shape[0]
    width = latent_rows.shape[1]
    row_first = lax.axis_index("rows") * height
    col_first = 0
    total_rows = height * lax.axis_size("rows")
    latent_pad = with_halo(latent_rows, (("rows", 0),), 3)
    latent_pad = jnp.pad(latent_pad, ((0, 0), (3, 3), (0, 0)))

    def pad_grad(field):
        padded = with_halo(field.astype(jnp.bfloat16), (("rows", 0),), 3).astype(field.dtype)
        return jnp.pad(padded, ((0, 0), (3, 3), (0, 0)))

    features, gradient = local_block(
        latent_pad,
        row_first,
        col_first,
        total_rows,
        width,
        pad_grad,
        time_rows,
        class_half,
        slope_image,
        scale_half,
        dw_kernel,
        dw_bias,
        ln_gain,
        ln_bias,
        up_weight,
        up_bias,
        down_weight,
        down_bias,
        full_channels,
    )
    gradient = lax.all_to_all(gradient, "rows", split_axis=1, concat_axis=0, tiled=True)
    return (features, gradient)


def solution(mesh):
    in_specs = (
        P("groups", "rows", "chan"),
        P("groups"),
        P("groups"),
        P(None, "chan"),
        P(),
        P(None, None, "chan"),
        P("chan"),
        P("chan"),
        P("chan"),
        P(None, "chan"),
        P("chan"),
        P("chan", None),
        P("chan"),
        P(),
    )
    out_specs = (P(("groups", "rows"), None, "chan"), P("groups", "rows", "chan"))
    return jax.shard_map(
        per_device, mesh=mesh, in_specs=in_specs, out_specs=out_specs, check_vma=False
    )
```

profile of v0, /device:TPU:0, one launch (start us, length us, event | category | flops | bytes accessed | tf_op | source)
XLA Modules:
  0.0 107.5 jit_solution(14234665979605698154)
XLA Ops:
  7.2 7.5 %all-to-all-start = ((bf16[24,4,512]{2,1,0:T(4,128)(2,1)}), bf16[24,4,512]{2,1,0:T(4,128)(2,1)S(1)}, u32[]{:S(2)}, u32[]{:S(2)}) async-start(bf16[24,4,512]{2,1,0:T(4,128)(2,1)} %param.14), calls=%async_computation | async-start | bytes 196608 | tf_op jit(solution)/shard_map/all_to_all | solution.py:188
  15.8 1.1 %fusion.183 = (f32[1,1,512]{2,1,0:T(1,128)S(1)}, f32[1,1,512]{2,1,0:T(1,128)S(1)}, f32[1,1,512]{2,1,0:T(1,128)S(1)}, f32[1,1,512]{2,1,0:T(1,128)S(1)}, f32[1,1,5...) fusion(bf16[7,7,512]{2,1,0:T(8,128)(2,1)} %param.19), kind=kLoop, calls=%fused_computation.314 | loop fusion | bytes 77824 | tf_op jit(solution)/shard_map/slice | solution.py:49
  17.1 1.6 %fusion.182 = (f32[1,1,512]{2,1,0:T(1,128)S(1)}, f32[1,1,512]{2,1,0:T(1,128)S(1)}, f32[1,1,512]{2,1,0:T(1,128)S(1)}, f32[1,1,512]{2,1,0:T(1,128)S(1)}, f32[1,1,5...) fusion(bf16[7,7,512]{2,1,0:T(8,128)(2,1)} %param.19), kind=kLoop, calls=%fused_computation.313 | loop fusion | bytes 77824 | tf_op jit(solution)/shard_map/slice | solution.py:49
  23.7 3.4 %fusion.164 = f32[3,2048]{1,0:T(4,128)S(1)} fusion(bf16[2048,1024]{1,0:T(8,128)(2,1)} %param.25, f32[3,1024]{1,0:T(4,128)S(1)} %fusion.169, f32[1024]{0:T(1024)S(1)} %convert_element_type.93), kind=kOutput, calls=%fused_computation.280 | convolution fusion | flops 12589056 | bytes 4235264 | tf_op jit(solution)/shard_map/dot_general | solution.py:185
  28.0 1.3 %collective-permute-start.1 = (bf16[3,32,512]{2,0,1:T(4,128)(2,1)S(1)}, bf16[3,32,512]{2,0,1:T(4,128)(2,1)S(1)}, u32[]{:S(2)}, u32[]{:S(2)}) collective-permute-start(bf16[3,32,512]{2,0,1:T(4,128)(2,1)S(1)} %bitcast.86), channel_id=1, source_target_pairs={{2,0},{4,2},{6,4},{8,6},{10,8},{12,10},{14,12},{3,1},{5,3},{7,5},{... | collective-permute-start | bytes 294920 | tf_op jit(solution)/shard_map/ppermute | solution.py:20
  29.3 4.6 %collective-permute-start = (bf16[3,32,512]{2,0,1:T(4,128)(2,1)S(1)}, bf16[3,32,512]{2,0,1:T(4,128)(2,1)S(1)}, u32[]{:S(2)}, u32[]{:S(2)}) collective-permute-start(bf16[3,32,512]{2,0,1:T(4,128)(2,1)S(1)} %bitcast.87), channel_id=1, source_target_pairs={{0,2},{2,4},{4,6},{6,8},{8,10},{10,12},{12,14},{1,3},{3,5},{5,7},{... | collective-permute-start | bytes 294920 | tf_op jit(solution)/shard_map/ppermute | solution.py:18
  33.9 1.0 collective-permute-done.1
  34.9 2.9 %collective-permute-done = bf16[3,32,512]{2,0,1:T(4,128)(2,1)S(1)} collective-permute-done((bf16[3,32,512]{2,0,1:T(4,128)(2,1)S(1)}, bf16[3,32,512]{2,0,1:T(4,128)(2,1)S(1)}, u32[]{:S(2)}, u32[]{:S(2)}) %collective-permute-start) | collective-permute-done | bytes 98336 | tf_op jit(solution)/shard_map/ppermute | solution.py:18
  38.6 5.1 %fusion.180 = (f32[3,32]{0,1:T(8,128)S(1)}, f32[3,32]{0,1:T(8,128)S(1)}, f32[3,32,512]{2,0,1:T(4,128)S(1)}) fusion(f32[512]{0:T(512)S(1)} %convert_element_type.101, f32[3]{0:T(128)} %get-tuple-element.67, f32[512]{0:T(512)S(1)} %bitcast.113, f32[9,38,512]{2,0,1:T(8,128)S(1)} %multiply_add_fusion, f32[512]{0:T(512)S(1)} %bitcast.111, f32[512]{0:T(512)S(1)} %bitcast.109, ...), kind=kLoop, calls=%fused_computation.312 | loop fusion | flops 5259072 | bytes 9933640 | tf_op jit(solution)/shard_map/reduce_sum | solution.py:106
  44.0 2.5 %all-reduce.3 = (f32[96]{0:T(128)S(1)}, f32[96]{0:T(128)S(1)}) all-reduce(f32[96]{0:T(128)S(1)} %reduce_sum.43, f32[96]{0:T(128)S(1)} %reduce_sum.41), channel_id=1, replica_groups=mesh['groups'=2,'rows'=8,'chan'=2] {'chan'}, use_global_device_ids=true, to_apply=%region_3.4 | all-reduce | flops 192 | bytes 1536 | tf_op jit(solution)/shard_map/psum | solution.py:106
  46.6 1.9 %all_gather.3 = bf16[96,1024]{1,0:T(8,128)(2,1)S(1)} all-gather(bf16[96,512]{1,0:T(8,128)(2,1)S(1)} %add_convert_fusion), channel_id=1, replica_groups=mesh['groups'=2,'rows'=8,'chan'=2] {'chan'}, dimensions={1}, use_global_device_ids=true | all-gather | bytes 294912 | tf_op jit(solution)/shard_map/all_gather | solution.py:114
  48.6 3.6 %fusion.7 = (bf16[96,2048]{1,0:T(8,128)(2,1)S(1)}, f32[96,2048]{1,0:T(8,128)S(1)}) fusion(f32[3,2048]{1,0:T(4,128)S(1)} %fusion.171, f32[2048]{0:T(1024)S(1)} %convert_element_type.105, bf16[96,1024]{1,0:T(8,128)(2,1)S(1)} %all_gather.3, bf16[1024,2048]{1,0:T(8,128)(2,1)} %param.23), kind=kOutput, calls=%fused_computation.56 | convolution fusion | flops 406585344 | bytes 5603328 | tf_op jit(solution)/shard_map/dot_general | solution.py:113
  52.2 2.1 %convolution_convert_fusion = bf16[96,1024]{1,0:T(8,128)(2,1)} fusion(bf16[96,2048]{1,0:T(8,128)(2,1)S(1)} %get-tuple-element.68, bf16[1024,2048]{1,0:T(8,128)(2,1)S(1)} %copy-done.1), kind=kOutput, calls=%fused_computation.49 | convolution fusion | flops 402751488 | bytes 4784128 | tf_op jit(solution)/shard_map/dot_general | solution.py:137
  54.5 9.4 %reduce-scatter.5.cloned.1.call-done = bf16[96,512]{1,0:T(8,128)(2,1)} async-done(((bf16[96,1024]{1,0:T(8,128)(2,1)}), bf16[96,512]{1,0:T(8,128)(2,1)}) %reduce-scatter.5.cloned.1.call-update) | async-done | bytes 98320 | tf_op jit(solution)/shard_map/reduce_scatter | solution.py:140
  63.9 1.1 %fusion.162 = (f32[96]{0:T(128)S(1)}, f32[96]{0:T(128)S(1)}) fusion(bf16[96,512]{1,0:T(8,128)(2,1)} %reduce-scatter.5.cloned.1.call-done, f32[512]{0:T(512)S(1)} %convert_element_type.102, f32[96]{0:T(128)S(1)} %get-tuple-element.61, f32[96]{0:T(128)S(1)} %get-tuple-element.60, f32[3,32,512]{2,1,0:T(8,128)S(1)} %copy.27), kind=kLoop, calls=%fused_computation.275 | loop fusion | flops 343872 | bytes 298496 | tf_op jit(solution)/shard_map/reduce_sum | solution.py:144
  65.0 2.5 %all-reduce.2 = (f32[96]{0:T(128)S(1)}, f32[96]{0:T(128)S(1)}) all-reduce(f32[96]{0:T(128)S(1)} %get-tuple-element.5, f32[96]{0:T(128)S(1)} %get-tuple-element.4), channel_id=1, replica_groups=mesh['groups'=2,'rows'=8,'chan'=2] {'chan'}, use_global_device_ids=true, to_apply=%region_9.10 | all-reduce | flops 192 | bytes 1536 | tf_op jit(solution)/shard_map/psum | solution.py:144
  67.5 1.0 multiply_convert_fusion.2
  68.6 1.3 %collective-permute-start.3 = (bf16[3,32,512]{2,0,1:T(4,128)(2,1)S(1)}, bf16[3,32,512]{2,0,1:T(4,128)(2,1)S(1)}, u32[]{:S(2)}, u32[]{:S(2)}) collective-permute-start(bf16[3,32,512]{2,0,1:T(4,128)(2,1)S(1)} %copy.30), channel_id=1, source_target_pairs={{2,0},{4,2},{6,4},{8,6},{10,8},{12,10},{14,12},{3,1},{5,3},{7,5},{... | collective-permute-start | bytes 294920 | tf_op jit(solution)/shard_map/ppermute | solution.py:20
  69.9 4.6 %collective-permute-start.2 = (bf16[3,32,512]{2,0,1:T(4,128)(2,1)S(1)}, bf16[3,32,512]{2,0,1:T(4,128)(2,1)S(1)}, u32[]{:S(2)}, u32[]{:S(2)}) collective-permute-start(bf16[3,32,512]{2,0,1:T(4,128)(2,1)S(1)} %copy.30), channel_id=1, source_target_pairs={{0,2},{2,4},{4,6},{6,8},{8,10},{10,12},{12,14},{1,3},{3,5},{5,7},{... | collective-permute-start | bytes 294920 | tf_op jit(solution)/shard_map/ppermute | solution.py:18
  74.5 3.8 %fusion.13 = f32[96,1024]{1,0:T(8,128)} fusion(bf16[2048,1024]{1,0:T(8,128)(2,1)} %param.25, f32[96,2048]{1,0:T(8,128)S(1)} %get-tuple-element.69), kind=kOutput, calls=%fused_computation.64 | convolution fusion | flops 404422656 | bytes 5373952 | tf_op jit(solution)/shard_map/dot_general | solution.py:121
  79.9 5.3 %add_add_fusion = f32[3,32,512]{2,0,1:T(4,128)} fusion(f32[9,32,512]{2,0,1:T(8,128)S(1)} %maximum_convert_fusion, f32[3,512]{1,0:T(4,128)S(1)} %fusion.165, f32[3]{0:T(128)} %get-tuple-element.67, f32[512]{0:T(512)S(1)} %bitcast.114, f32[512]{0:T(512)S(1)} %bitcast.112, f32[512]{0:T(512)S(1)} %bitcast.110, f32[512]{0:T(512)S(1)} %bitcast.108, ...), kind=kLoop, calls=%fused_computation.266 | loop fusion | flops 5111808 | bytes 3188808 | tf_op jit(solution)/shard_map/add | solution.py:150
  85.2 5.9 %all-to-all-start.1 = ((f32[3,32,512]{2,0,1:T(4,128)}), f32[3,32,512]{2,0,1:T(4,128)S(1)}, u32[]{:S(2)}, u32[]{:S(2)}) async-start(f32[3,32,512]{2,0,1:T(4,128)} %add_add_fusion), calls=%async_computation.3 | async-start | bytes 524288 | tf_op jit(solution)/shard_map/all_to_all | solution.py:222
  92.1 1.6 %fusion.161 = bf16[96,512]{1,0:T(8,128)(2,1)} fusion(f32[3,32,512]{2,1,0:T(8,128)S(1)} %copy.26, f32[96,512]{1,0:T(8,128)} %reduce-scatter.3.cloned.1.call-done, f32[512]{0:T(512)S(1)} %convert_element_type.107, f32[512]{0:T(512)S(1)} %dynamic_slice.6), kind=kLoop, calls=%fused_computation.271 | loop fusion | flops 196608 | bytes 495616 | tf_op jit(solution)/shard_map/convert_element_type | solution.py:129
  93.7 6.3 %all-to-all-done.1 = f32[3,32,512]{2,0,1:T(4,128)S(1)} async-done(((f32[3,32,512]{2,0,1:T(4,128)}), f32[3,32,512]{2,0,1:T(4,128)S(1)}, u32[]{:S(2)}, u32[]{:S(2)}) %all-to-all-start.1) | async-done | bytes 196640 | tf_op jit(solution)/shard_map/all_to_all | solution.py:222
  (206 shorter events, 10.7 us)
Async XLA Ops:
  7.2 20.8 %all-to-all-start = ((bf16[24,4,512]{2,1,0:T(4,128)(2,1)}), bf16[24,4,512]{2,1,0:T(4,128)(2,1)S(1)}, u32[]{:S(2)}, u32[]{:S(2)}) async-start(bf16[24,4,512]{2,1,0:T(4,128)(2,1)} %param.14), calls=%async_computation | async-start | bytes 196608 | tf_op jit(solution)/shard_map/all_to_all | solution.py:188
  14.7 49.3 %reduce-scatter.5.cloned.1.call-start = ((), (), s32[]{:S(2)}) async-start(), calls=%async_computation.5 | async-start | bytes 294912 | tf_op jit(solution)/shard_map/reduce_scatter | solution.py:140
  15.7 22.5 %copy-start.2 = (f32[1,1,512]{2,1,0:T(1,128)}, f32[1,1,512]{2,1,0:T(1,128)S(1)}, u32[]{:S(2)}) copy-start(f32[1,1,512]{2,1,0:T(1,128)S(1)} %get-tuple-element.51) | copy-start | bytes 6148
  15.7 22.5 %copy-start.4 = (f32[1,1,512]{2,1,0:T(1,128)}, f32[1,1,512]{2,1,0:T(1,128)S(1)}, u32[]{:S(2)}) copy-start(f32[1,1,512]{2,1,0:T(1,128)S(1)} %get-tuple-element.52) | copy-start | bytes 6148
  15.7 22.5 %copy-start.6 = (f32[1,1,512]{2,1,0:T(1,128)}, f32[1,1,512]{2,1,0:T(1,128)S(1)}, u32[]{:S(2)}) copy-start(f32[1,1,512]{2,1,0:T(1,128)S(1)} %get-tuple-element.53) | copy-start | bytes 6148
  15.7 22.5 %copy-start.8 = (f32[1,1,512]{2,1,0:T(1,128)}, f32[1,1,512]{2,1,0:T(1,128)S(1)}, u32[]{:S(2)}) copy-start(f32[1,1,512]{2,1,0:T(1,128)S(1)} %get-tuple-element.54) | copy-start | bytes 6148
  15.7 22.5 %copy-start.10 = (f32[1,1,512]{2,1,0:T(1,128)}, f32[1,1,512]{2,1,0:T(1,128)S(1)}, u32[]{:S(2)}) copy-start(f32[1,1,512]{2,1,0:T(1,128)S(1)} %get-tuple-element.55) | copy-start | bytes 6148
  15.7 22.5 %copy-start.12 = (f32[1,1,512]{2,1,0:T(1,128)}, f32[1,1,512]{2,1,0:T(1,128)S(1)}, u32[]{:S(2)}) copy-start(f32[1,1,512]{2,1,0:T(1,128)S(1)} %get-tuple-element.56) | copy-start | bytes 6148
  15.7 22.5 %copy-start.14 = (f32[1,1,512]{2,1,0:T(1,128)}, f32[1,1,512]{2,1,0:T(1,128)S(1)}, u32[]{:S(2)}) copy-start(f32[1,1,512]{2,1,0:T(1,128)S(1)} %get-tuple-element.57) | copy-start | bytes 6148
  15.8 22.5 %copy-start.16 = (f32[1,1,512]{2,1,0:T(1,128)}, f32[1,1,512]{2,1,0:T(1,128)S(1)}, u32[]{:S(2)}) copy-start(f32[1,1,512]{2,1,0:T(1,128)S(1)} %get-tuple-element.58) | copy-start | bytes 6148
  15.8 22.5 %copy-start.18 = (f32[1,1,512]{2,1,0:T(1,128)}, f32[1,1,512]{2,1,0:T(1,128)S(1)}, u32[]{:S(2)}) copy-start(f32[1,1,512]{2,1,0:T(1,128)S(1)} %get-tuple-element.59) | copy-start | bytes 6148
  16.9 21.3 %copy-start.20 = (f32[1,1,512]{2,1,0:T(1,128)}, f32[1,1,512]{2,1,0:T(1,128)S(1)}, u32[]{:S(2)}) copy-start(f32[1,1,512]{2,1,0:T(1,128)S(1)} %get-tuple-element.30) | copy-start | bytes 6148
  16.9 21.3 %copy-start.22 = (f32[1,1,512]{2,1,0:T(1,128)}, f32[1,1,512]{2,1,0:T(1,128)S(1)}, u32[]{:S(2)}) copy-start(f32[1,1,512]{2,1,0:T(1,128)S(1)} %get-tuple-element.31) | copy-start | bytes 6148
  16.9 21.3 %copy-start.24 = (f32[1,1,512]{2,1,0:T(1,128)}, f32[1,1,512]{2,1,0:T(1,128)S(1)}, u32[]{:S(2)}) copy-start(f32[1,1,512]{2,1,0:T(1,128)S(1)} %get-tuple-element.32) | copy-start | bytes 6148
  16.9 21.3 %copy-start.26 = (f32[1,1,512]{2,1,0:T(1,128)}, f32[1,1,512]{2,1,0:T(1,128)S(1)}, u32[]{:S(2)}) copy-start(f32[1,1,512]{2,1,0:T(1,128)S(1)} %get-tuple-element.33) | copy-start | bytes 6148
  17.0 21.3 %copy-start.28 = (f32[1,1,512]{2,1,0:T(1,128)}, f32[1,1,512]{2,1,0:T(1,128)S(1)}, u32[]{:S(2)}) copy-start(f32[1,1,512]{2,1,0:T(1,128)S(1)} %get-tuple-element.34) | copy-start | bytes 6148
  17.0 21.3 %copy-start.30 = (f32[1,1,512]{2,1,0:T(1,128)}, f32[1,1,512]{2,1,0:T(1,128)S(1)}, u32[]{:S(2)}) copy-start(f32[1,1,512]{2,1,0:T(1,128)S(1)} %get-tuple-element.35) | copy-start | bytes 6148
  17.0 21.3 %copy-start.32 = (f32[1,1,512]{2,1,0:T(1,128)}, f32[1,1,512]{2,1,0:T(1,128)S(1)}, u32[]{:S(2)}) copy-start(f32[1,1,512]{2,1,0:T(1,128)S(1)} %get-tuple-element.36) | copy-start | bytes 6148
  28.0 6.9 %collective-permute-start.1 = (bf16[3,32,512]{2,0,1:T(4,128)(2,1)S(1)}, bf16[3,32,512]{2,0,1:T(4,128)(2,1)S(1)}, u32[]{:S(2)}, u32[]{:S(2)}) collective-permute-start(bf16[3,32,512]{2,0,1:T(4,128)(2,1)S(1)} %bitcast.86), channel_id=1, source_target_pairs={{2,0},{4,2},{6,4},{8,6},{10,8},{12,10},{14,12},{3,1},{5,3},{7,5},{... | collective-permute-start | bytes 294920 | tf_op jit(solution)/shard_map/ppermute | solution.py:20
  29.3 8.5 %collective-permute-start = (bf16[3,32,512]{2,0,1:T(4,128)(2,1)S(1)}, bf16[3,32,512]{2,0,1:T(4,128)(2,1)S(1)}, u32[]{:S(2)}, u32[]{:S(2)}) collective-permute-start(bf16[3,32,512]{2,0,1:T(4,128)(2,1)S(1)} %bitcast.87), channel_id=1, source_target_pairs={{0,2},{2,4},{4,6},{6,8},{8,10},{10,12},{12,14},{1,3},{3,5},{5,7},{... | collective-permute-start | bytes 294920 | tf_op jit(solution)/shard_map/ppermute | solution.py:18
  54.3 37.8 %reduce-scatter.3.cloned.1.call-start = ((), (), s32[]{:S(2)}) async-start(), calls=%async_computation.4 | async-start | bytes 589824 | tf_op jit(solution)/shard_map/reduce_scatter | solution.py:120
  68.6 10.1 %collective-permute-start.3 = (bf16[3,32,512]{2,0,1:T(4,128)(2,1)S(1)}, bf16[3,32,512]{2,0,1:T(4,128)(2,1)S(1)}, u32[]{:S(2)}, u32[]{:S(2)}) collective-permute-start(bf16[3,32,512]{2,0,1:T(4,128)(2,1)S(1)} %copy.30), channel_id=1, source_target_pairs={{2,0},{4,2},{6,4},{8,6},{10,8},{12,10},{14,12},{3,1},{5,3},{7,5},{... | collective-permute-start | bytes 294920 | tf_op jit(solution)/shard_map/ppermute | solution.py:20
  69.9 9.3 %collective-permute-start.2 = (bf16[3,32,512]{2,0,1:T(4,128)(2,1)S(1)}, bf16[3,32,512]{2,0,1:T(4,128)(2,1)S(1)}, u32[]{:S(2)}, u32[]{:S(2)}) collective-permute-start(bf16[3,32,512]{2,0,1:T(4,128)(2,1)S(1)} %copy.30), channel_id=1, source_target_pairs={{0,2},{2,4},{4,6},{6,8},{8,10},{10,12},{12,14},{1,3},{3,5},{5,7},{... | collective-permute-start | bytes 294920 | tf_op jit(solution)/shard_map/ppermute | solution.py:18
  85.2 14.7 %all-to-all-start.1 = ((f32[3,32,512]{2,0,1:T(4,128)}), f32[3,32,512]{2,0,1:T(4,128)S(1)}, u32[]{:S(2)}, u32[]{:S(2)}) async-start(f32[3,32,512]{2,0,1:T(4,128)} %add_add_fusion), calls=%async_computation.3 | async-start | bytes 524288 | tf_op jit(solution)/shard_map/all_to_all | solution.py:222
  (67 other events, 582.4 us)
Sparse Core Ops, SparseCore 0:
  54.4 9.4 reduce-scatter.4
  78.8 8.9 reduce-scatter.2
where the time goes:
time: 109 us; the launch traced here: 108 us
  starting transfers between devices  25.1 us (23%)
  waiting for transfers between devices  20.2 us (19%)
  other arithmetic  19.8 us (18%)
  between operations  15.5 us (14%)
  matrix products  14.5 us (13%)
  blocking collectives  6.89 us (6%)
  local copies, waits for them, and re-layouts  5.62 us (5%)
    reduce_scatter x1, waiting for transfers between devices, local_block(): lax.psum_scatter(grad_terms.astype(jnp.bfloat16), 'chan', scatter_dimensi...  9.45 us
    ppermute x2, starting transfers between devices, with_halo(): lax.ppermute(tail, axis, [(i, (i + 1) % count) for i in range(ends)])  9.11 us
    all_to_all x1, starting transfers between devices, per_device(): lax.all_to_all(latents, 'rows', split_axis=0, concat_axis=1, tiled=True)  7.45 us
    all_to_all x1, waiting for transfers between devices, per_device(): lax.all_to_all(gradient, 'rows', split_axis=1, concat_axis=0, tiled=True)  6.28 us
    all_to_all x1, starting transfers between devices, per_device(): lax.all_to_all(gradient, 'rows', split_axis=1, concat_axis=0, tiled=True)  5.88 us
    add x1, other arithmetic, local_block(): stencil(grad_pad, kernel[::-1, ::-1], masks) + class_tokens[:, None, :]  5.34 us
    reduce_sum x1, other arithmetic, local_block(): jnp.sum(flat, 1)  5.05 us
    dot_general x1, matrix products, local_block(): jnp.dot(active, down_weight, preferred_element_type=jnp.float32)  3.82 us
  transfers between devices with their start and end apart: 8, of which 5 were waited for; matrix products, arithmetic and copies ran while one was open for 23% of the time, Pallas kernels for 0%

commit v1 on v0

--- a/solution.py
+++ b/solution.py
@@ -185,7 +185,10 @@
     slope_image = lax.dot_general(
         direction, down_weight, (((1,), (1,)), ((), ())), preferred_element_type=jnp.float32
     )
-    latent_rows = lax.all_to_all(latents, "rows", split_axis=0, concat_axis=1, tiled=True)
+    latent_rows = jnp.concatenate(
+        lax.all_to_all(jnp.stack(jnp.split(latents, lax.axis_size("rows"), axis=0)), "rows", 0, 0),
+        axis=1,
+    )
     height = latent_rows.shape[0]
     width = latent_rows.shape[1]
     row_first = lax.axis_index("rows") * height

time: 109 us -> 109 us (level)
  local copies, waits for them, and re-layouts: 5.62 us -> 15.9 us
  other arithmetic: 19.8 us -> 10.7 us
  between operations: 15.5 us -> 14.2 us
    unnamed x166 -> x15, local copies, waits for them, and re-layouts: 0.36 us -> 9.3 us
    add x1, other arithmetic: 5.34 us -> 1.19 us  [local_block(): stencil(grad_pad, kernel[::-1, ::-1], masks) + class_tokens[:, None, :]]
    reduce_sum x1, other arithmetic: 5.05 us -> 1.85 us  [local_block(): jnp.sum(flat, 1)]
    reduce_scatter x1, waiting for transfers between devices: 9.45 us -> 6.76 us  [local_block(): lax.psum_scatter(grad_terms.astype(jnp.bfloat16), 'chan', scatter_dimensi...]
    another operation x0 -> x1, local copies, waits for them, and re-layouts: none -> 1.31 us  [per_device(): jnp.stack(jnp.split(latents, lax.axis_size('rows'), axis=0))]
  transfers between devices with their start and end apart: 8 -> 8, of which waited for: 5 -> 6; matrix products, arithmetic and copies ran while one was open for 23% -> 21% of each run, Pallas kernels for 0% -> 0%
where the time goes in v1:
time: 109 us; the launch traced here: 108 us
  starting transfers between devices  25.7 us (24%)
  waiting for transfers between devices  19.2 us (18%)
  local copies, waits for them, and re-layouts  15.9 us (15%)
  matrix products  15.1 us (14%)
  between operations  14.2 us (13%)
  other arithmetic  10.7 us (10%)
  blocking collectives  7 us (6%)
    unnamed x15, local copies, waits for them, and re-layouts  9.3 us
    ppermute x2, starting transfers between devices, with_halo(): lax.ppermute(tail, axis, [(i, (i + 1) % count) for i in range(ends)])  9.1 us
    all_to_all x1, starting transfers between devices, per_device(): lax.all_to_all(jnp.stack(jnp.split(latents, lax.axis_size('rows'), axis=0...  7.31 us
    reduce_scatter x1, waiting for transfers between devices, local_block(): lax.psum_scatter(grad_terms.astype(jnp.bfloat16), 'chan', scatter_dimensi...  6.76 us
    all_to_all x1, waiting for transfers between devices, per_device(): lax.all_to_all(gradient, 'rows', split_axis=1, concat_axis=0, tiled=True)  6.69 us
    all_to_all x1, starting transfers between devices, per_device(): lax.all_to_all(gradient, 'rows', split_axis=1, concat_axis=0, tiled=True)  6.58 us
    ppermute x2, waiting for transfers between devices, with_halo(): lax.ppermute(tail, axis, [(i, (i + 1) % count) for i in range(ends)])  4.13 us
    dot_general x1, matrix products, local_block(): jnp.dot(active, down_weight, preferred_element_type=jnp.float32)  3.81 us
  transfers between devices with their start and end apart: 8, of which 6 were waited for; matrix products, arithmetic and copies ran while one was open for 21% of the time, Pallas kernels for 0%

profile of v1, /device:TPU:0, one launch (start us, length us, event | category | flops | bytes accessed | tf_op | source)
XLA Modules:
  0.0 107.8 jit_solution(15557042042113184184)
XLA Ops:
  7.2 1.4 %constant_dynamic-update-slice_fusion.7 = bf16[8,3,4,512]{3,2,1,0:T(4,128)(2,1)} fusion(bf16[24,4,512]{2,1,0:T(4,128)(2,1)} %param.14), kind=kLoop, calls=%fused_computation.293 | loop fusion | bytes 24576
  8.6 1.3 %constant_dynamic-update-slice_fusion.6 = bf16[8,3,4,512]{3,2,1,0:T(4,128)(2,1)} fusion(bf16[8,3,4,512]{3,2,1,0:T(4,128)(2,1)} %constant_dynamic-update-slice_fusion.7, bf16[24,4,512]{2,1,0:T(4,128)(2,1)} %param.14), kind=kLoop, calls=%fused_computation.292 | loop fusion | bytes 24576
  9.9 1.3 %constant_dynamic-update-slice_fusion.5 = bf16[8,3,4,512]{3,2,1,0:T(4,128)(2,1)} fusion(bf16[8,3,4,512]{3,2,1,0:T(4,128)(2,1)} %constant_dynamic-update-slice_fusion.6, bf16[24,4,512]{2,1,0:T(4,128)(2,1)} %param.14), kind=kLoop, calls=%fused_computation.291 | loop fusion | bytes 24576
  11.2 1.3 %constant_dynamic-update-slice_fusion.4 = bf16[8,3,4,512]{3,2,1,0:T(4,128)(2,1)} fusion(bf16[8,3,4,512]{3,2,1,0:T(4,128)(2,1)} %constant_dynamic-update-slice_fusion.5, bf16[24,4,512]{2,1,0:T(4,128)(2,1)} %param.14), kind=kLoop, calls=%fused_computation.290 | loop fusion | bytes 24576
  12.5 1.3 %constant_dynamic-update-slice_fusion.3 = bf16[8,3,4,512]{3,2,1,0:T(4,128)(2,1)} fusion(bf16[8,3,4,512]{3,2,1,0:T(4,128)(2,1)} %constant_dynamic-update-slice_fusion.4, bf16[24,4,512]{2,1,0:T(4,128)(2,1)} %param.14), kind=kLoop, calls=%fused_computation.289 | loop fusion | bytes 24576
  13.8 1.3 %constant_dynamic-update-slice_fusion.2 = bf16[8,3,4,512]{3,2,1,0:T(4,128)(2,1)} fusion(bf16[8,3,4,512]{3,2,1,0:T(4,128)(2,1)} %constant_dynamic-update-slice_fusion.3, bf16[24,4,512]{2,1,0:T(4,128)(2,1)} %param.14), kind=kLoop, calls=%fused_computation.288 | loop fusion | bytes 24576
  15.1 1.3 %constant_dynamic-update-slice_fusion.1 = bf16[8,3,4,512]{3,2,1,0:T(4,128)(2,1)} fusion(bf16[8,3,4,512]{3,2,1,0:T(4,128)(2,1)} %constant_dynamic-update-slice_fusion.2, bf16[24,4,512]{2,1,0:T(4,128)(2,1)} %param.14), kind=kLoop, calls=%fused_computation.287 | loop fusion | bytes 24576
  17.8 7.3 %all-to-all-start = ((bf16[8,3,4,512]{3,2,1,0:T(4,128)(2,1)}), bf16[8,3,4,512]{3,2,1,0:T(4,128)(2,1)S(1)}, u32[]{:S(2)}, u32[]{:S(2)}) async-start(bf16[8,3,4,512]{3,2,1,0:T(4,128)(2,1)} %constant_dynamic-update-slice_fusion), calls=%async_computation | async-start | bytes 196608 | tf_op jit(solution)/shard_map/all_to_all | solution.py:189
  34.1 3.4 %fusion.174 = f32[3,2048]{1,0:T(4,128)S(1)} fusion(bf16[2048,1024]{1,0:T(8,128)(2,1)} %param.25, f32[3,1024]{1,0:T(4,128)S(1)} %fusion.179, f32[1024]{0:T(1024)S(1)} %convert_element_type.93), kind=kOutput, calls=%fused_computation.297 | convolution fusion | flops 12589056 | bytes 4235264 | tf_op jit(solution)/shard_map/dot_general | solution.py:185
  39.1 4.6 %collective-permute-start = (bf16[3,32,512]{2,1,0:T(8,128)(2,1)S(1)}, bf16[3,32,512]{2,1,0:T(8,128)(2,1)S(1)}, u32[]{:S(2)}, u32[]{:S(2)}) collective-permute-start(bf16[3,32,512]{2,1,0:T(8,128)(2,1)S(1)} %reshape.77), channel_id=1, source_target_pairs={{0,2},{2,4},{4,6},{6,8},{8,10},{10,12},{12,14},{1,3},{3,5},{5,7},{... | collective-permute-start | bytes 294920 | tf_op jit(solution)/shard_map/ppermute | solution.py:18
  44.3 1.9 %collective-permute-done = bf16[3,32,512]{2,1,0:T(8,128)(2,1)S(1)} collective-permute-done((bf16[3,32,512]{2,1,0:T(8,128)(2,1)S(1)}, bf16[3,32,512]{2,1,0:T(8,128)(2,1)S(1)}, u32[]{:S(2)}, u32[]{:S(2)}) %collective-permute-start) | collective-permute-done | bytes 98336 | tf_op jit(solution)/shard_map/ppermute | solution.py:18
  46.3 1.8 %fusion.190 = (f32[3,32]{1,0:T(4,128)S(1)}, f32[3,32]{1,0:T(4,128)S(1)}, f32[3,32,512]{2,1,0:T(8,128)S(1)}) fusion(f32[512]{0:T(512)S(1)} %convert_element_type.101, f32[3]{0:T(128)S(1)} %get-tuple-element.67, f32[512]{0:T(512)S(1)} %bitcast.125, f32[9,38,512]{2,1,0:T(8,128)S(1)} %multiply_add_fusion.1, f32[512]{0:T(512)S(1)} %bitcast.123, ...), kind=kLoop, calls=%fused_computation.329 | loop fusion | flops 5259072 | bytes 9933640 | tf_op jit(solution)/shard_map/reduce_sum | solution.py:106
  48.4 2.5 %all-reduce.3 = (f32[96]{0:T(128)S(1)}, f32[96]{0:T(128)S(1)}) all-reduce(f32[96]{0:T(128)S(1)} %reduce_sum.43, f32[96]{0:T(128)S(1)} %reduce_sum.41), channel_id=1, replica_groups=mesh['groups'=2,'rows'=8,'chan'=2] {'chan'}, use_global_device_ids=true, to_apply=%region_3.4 | all-reduce | flops 192 | bytes 1536 | tf_op jit(solution)/shard_map/psum | solution.py:106
  50.9 2.1 %all_gather.3 = bf16[96,1024]{1,0:T(8,128)(2,1)S(1)} all-gather(bf16[96,512]{1,0:T(8,128)(2,1)S(1)} %add_convert_fusion), channel_id=1, replica_groups=mesh['groups'=2,'rows'=8,'chan'=2] {'chan'}, dimensions={1}, use_global_device_ids=true | all-gather | bytes 294912 | tf_op jit(solution)/shard_map/all_gather | solution.py:114
  53.0 3.4 %fusion.6 = (bf16[96,2048]{1,0:T(8,128)(2,1)S(1)}, f32[96,2048]{1,0:T(8,128)S(1)}) fusion(f32[3,2048]{1,0:T(4,128)S(1)} %fusion.181, f32[2048]{0:T(1024)S(1)} %convert_element_type.105, bf16[96,1024]{1,0:T(8,128)(2,1)S(1)} %all_gather.3, bf16[1024,2048]{1,0:T(8,128)(2,1)} %param.23), kind=kOutput, calls=%fused_computation.54 | convolution fusion | flops 406585344 | bytes 5603328 | tf_op jit(solution)/shard_map/dot_general | solution.py:113
  56.5 2.1 %convolution_convert_fusion = bf16[96,1024]{1,0:T(8,128)(2,1)} fusion(bf16[96,2048]{1,0:T(8,128)(2,1)S(1)} %get-tuple-element.68, bf16[1024,2048]{1,0:T(8,128)(2,1)S(1)} %copy-done.1), kind=kOutput, calls=%fused_computation.45 | convolution fusion | flops 402751488 | bytes 4784128 | tf_op jit(solution)/shard_map/dot_general | solution.py:137
  58.7 3.8 %fusion.11 = f32[96,1024]{1,0:T(8,128)} fusion(bf16[2048,1024]{1,0:T(8,128)(2,1)} %param.25, f32[96,2048]{1,0:T(8,128)S(1)} %get-tuple-element.69), kind=kOutput, calls=%fused_computation.61 | convolution fusion | flops 404422656 | bytes 5373952 | tf_op jit(solution)/shard_map/dot_general | solution.py:121
  62.5 6.8 %reduce-scatter.5.cloned.1.call-done = bf16[96,512]{1,0:T(8,128)(2,1)} async-done(((bf16[96,1024]{1,0:T(8,128)(2,1)}), bf16[96,512]{1,0:T(8,128)(2,1)}) %reduce-scatter.5.cloned.1.call-update) | async-done | bytes 98320 | tf_op jit(solution)/shard_map/reduce_scatter | solution.py:140
  70.4 2.5 %all-reduce.2 = (f32[96]{0:T(128)S(1)}, f32[96]{0:T(128)S(1)}) all-reduce(f32[96]{0:T(128)S(1)} %get-tuple-element.5, f32[96]{0:T(128)S(1)} %get-tuple-element.4), channel_id=1, replica_groups=mesh['groups'=2,'rows'=8,'chan'=2] {'chan'}, use_global_device_ids=true, to_apply=%region_9.10 | all-reduce | flops 192 | bytes 1536 | tf_op jit(solution)/shard_map/psum | solution.py:144
  75.2 4.6 %collective-permute-start.2 = (bf16[3,32,512]{2,1,0:T(8,128)(2,1)S(1)}, bf16[3,32,512]{2,1,0:T(8,128)(2,1)S(1)}, u32[]{:S(2)}, u32[]{:S(2)}) collective-permute-start(bf16[3,32,512]{2,1,0:T(8,128)(2,1)S(1)} %bitcast.101), channel_id=1, source_target_pairs={{0,2},{2,4},{4,6},{6,8},{8,10},{10,12},{12,14},{1,3},{3,5},{5,7},{... | collective-permute-start | bytes 294920 | tf_op jit(solution)/shard_map/ppermute | solution.py:18
  80.8 2.3 %collective-permute-done.2 = bf16[3,32,512]{2,1,0:T(8,128)(2,1)S(1)} collective-permute-done((bf16[3,32,512]{2,1,0:T(8,128)(2,1)S(1)}, bf16[3,32,512]{2,1,0:T(8,128)(2,1)S(1)}, u32[]{:S(2)}, u32[]{:S(2)}) %collective-permute-start.2) | collective-permute-done | bytes 98336 | tf_op jit(solution)/shard_map/ppermute | solution.py:18
  85.1 6.6 %all-to-all-start.1 = ((f32[3,32,512]{2,0,1:T(4,128)}), f32[3,32,512]{2,0,1:T(4,128)S(1)}, u32[]{:S(2)}, u32[]{:S(2)}) async-start(f32[3,32,512]{2,0,1:T(4,128)} %copy.20), calls=%async_computation.3 | async-start | bytes 524288 | tf_op jit(solution)/shard_map/all_to_all | solution.py:225
  91.9 1.6 %fusion.170 = bf16[96,512]{1,0:T(8,128)(2,1)} fusion(f32[3,32,512]{2,1,0:T(8,128)S(1)} %slice.733, f32[96,512]{1,0:T(8,128)} %reduce-scatter.3.cloned.1.call-done, f32[512]{0:T(512)S(1)} %convert_element_type.107, f32[512]{0:T(512)S(1)} %dynamic_slice.6), kind=kLoop, calls=%fused_computation.278 | loop fusion | flops 196608 | bytes 495616 | tf_op jit(solution)/shard_map/convert_element_type | solution.py:129
  93.5 6.7 %all-to-all-done.1 = f32[3,32,512]{2,0,1:T(4,128)S(1)} async-done(((f32[3,32,512]{2,0,1:T(4,128)}), f32[3,32,512]{2,0,1:T(4,128)S(1)}, u32[]{:S(2)}, u32[]{:S(2)}) %all-to-all-start.1) | async-done | bytes 196640 | tf_op jit(solution)/shard_map/all_to_all | solution.py:225
  (53 shorter events, 20.5 us)
Async XLA Ops:
  7.2 24.8 %copy-start = (bf16[1000,512]{1,0:T(8,128)(2,1)S(1)}, bf16[1000,512]{1,0:T(8,128)(2,1)}, u32[]{:S(2)}) copy-start(bf16[1000,512]{1,0:T(8,128)(2,1)} %param.17) | copy-start | bytes 3072004
  17.8 19.9 %all-to-all-start = ((bf16[8,3,4,512]{3,2,1,0:T(4,128)(2,1)}), bf16[8,3,4,512]{3,2,1,0:T(4,128)(2,1)S(1)}, u32[]{:S(2)}, u32[]{:S(2)}) async-start(bf16[8,3,4,512]{3,2,1,0:T(4,128)(2,1)} %constant_dynamic-update-slice_fusion), calls=%async_computation | async-start | bytes 196608 | tf_op jit(solution)/shard_map/all_to_all | solution.py:189
  25.1 44.2 %reduce-scatter.5.cloned.1.call-start = ((), (), s32[]{:S(2)}) async-start(), calls=%async_computation.5 | async-start | bytes 294912 | tf_op jit(solution)/shard_map/reduce_scatter | solution.py:140
  37.8 6.5 %collective-permute-start.1 = (bf16[3,32,512]{2,1,0:T(8,128)(2,1)S(1)}, bf16[3,32,512]{2,1,0:T(8,128)(2,1)S(1)}, u32[]{:S(2)}, u32[]{:S(2)}) collective-permute-start(bf16[3,32,512]{2,1,0:T(8,128)(2,1)S(1)} %reshape.77), channel_id=1, source_target_pairs={{2,0},{4,2},{6,4},{8,6},{10,8},{12,10},{14,12},{3,1},{5,3},{7,5},{... | collective-permute-start | bytes 294920 | tf_op jit(solution)/shard_map/ppermute | solution.py:20
  39.1 7.1 %collective-permute-start = (bf16[3,32,512]{2,1,0:T(8,128)(2,1)S(1)}, bf16[3,32,512]{2,1,0:T(8,128)(2,1)S(1)}, u32[]{:S(2)}, u32[]{:S(2)}) collective-permute-start(bf16[3,32,512]{2,1,0:T(8,128)(2,1)S(1)} %reshape.77), channel_id=1, source_target_pairs={{0,2},{2,4},{4,6},{6,8},{8,10},{10,12},{12,14},{1,3},{3,5},{5,7},{... | collective-permute-start | bytes 294920 | tf_op jit(solution)/shard_map/ppermute | solution.py:18
  50.8 5.6 %copy-start.1 = (bf16[1024,2048]{1,0:T(8,128)(2,1)S(1)}, bf16[1024,2048]{1,0:T(8,128)(2,1)}, u32[]{:S(2)}) copy-start(bf16[1024,2048]{1,0:T(8,128)(2,1)} %param.23) | copy-start | bytes 12582916
  58.6 33.3 %reduce-scatter.3.cloned.1.call-start = ((), (), s32[]{:S(2)}) async-start(), calls=%async_computation.4 | async-start | bytes 589824 | tf_op jit(solution)/shard_map/reduce_scatter | solution.py:120
  58.7 33.1 %copy-start.2 = (bf16[1024]{0:T(1024)(128)(2,1)S(1)}, bf16[1024]{0:T(1024)(128)(2,1)}, u32[]{:S(2)}) copy-start(bf16[1024]{0:T(1024)(128)(2,1)} %param.27) | copy-start | bytes 6148
  58.7 33.1 %copy-start.3 = (bf16[512]{0:T(512)(128)(2,1)S(1)}, bf16[512]{0:T(512)(128)(2,1)}, u32[]{:S(2)}) copy-start(bf16[512]{0:T(512)(128)(2,1)} %param.26) | copy-start | bytes 3076
  73.9 6.9 %collective-permute-start.3 = (bf16[3,32,512]{2,1,0:T(8,128)(2,1)S(1)}, bf16[3,32,512]{2,1,0:T(8,128)(2,1)S(1)}, u32[]{:S(2)}, u32[]{:S(2)}) collective-permute-start(bf16[3,32,512]{2,1,0:T(8,128)(2,1)S(1)} %bitcast.100), channel_id=1, source_target_pairs={{2,0},{4,2},{6,4},{8,6},{10,8},{12,10},{14,12},{3,1},{5,3},{7,5},{... | collective-permute-start | bytes 294920 | tf_op jit(solution)/shard_map/ppermute | solution.py:20
  75.2 7.9 %collective-permute-start.2 = (bf16[3,32,512]{2,1,0:T(8,128)(2,1)S(1)}, bf16[3,32,512]{2,1,0:T(8,128)(2,1)S(1)}, u32[]{:S(2)}, u32[]{:S(2)}) collective-permute-start(bf16[3,32,512]{2,1,0:T(8,128)(2,1)S(1)} %bitcast.101), channel_id=1, source_target_pairs={{0,2},{2,4},{4,6},{6,8},{8,10},{10,12},{12,14},{1,3},{3,5},{5,7},{... | collective-permute-start | bytes 294920 | tf_op jit(solution)/shard_map/ppermute | solution.py:18
  85.1 15.0 %all-to-all-start.1 = ((f32[3,32,512]{2,0,1:T(4,128)}), f32[3,32,512]{2,0,1:T(4,128)S(1)}, u32[]{:S(2)}, u32[]{:S(2)}) async-start(f32[3,32,512]{2,0,1:T(4,128)} %copy.20), calls=%async_computation.3 | async-start | bytes 524288 | tf_op jit(solution)/shard_map/all_to_all | solution.py:225
Sparse Core Ops, SparseCore 0:
  58.7 10.5 reduce-scatter.4
  71.5 8.9 reduce-scatter.2
